TPU v7x, 256 devices: a whole 4x4x8 slice. The times are simulated.
256 devices in a mesh: row: 8 (over z_hi, y), col: 32 (over z_lo, x, core).
Axes of the slice: x: 4, y: 4, z: 8 (z_hi: 2, z_lo: 4; z = z_hi * 4 + z_lo), core: 2. Of those that a mesh axis runs over, the one named last changes fastest.
Arguments:
- inputs: bfloat16 [1024, 9216], P('col', 'row'), may hold values from -6 to 6
- out_grad: bfloat16 [1024, 9216], P('col', 'row'), may hold values from -6 to 6
- preact: bfloat16 [1024, 36864], P('row', 'col'), may hold values from -6 to 6
- first_weight: bfloat16 [9216, 36864], P('row', 'col'), may hold values from -0.0625 to 0.0625
- second_weight: bfloat16 [36864, 9216], P('col', 'row'), may hold values from -0.03125 to 0.03125
Outputs:
- grad_inputs: float32 [1024, 9216], P('col', 'row')
- grad_first: bfloat16 [9216, 36864], P('row', 'col')
- grad_second: bfloat16 [36864, 9216], P('col', 'row')
All inputs are finite; a program needn't handle non-finite values.
Results may differ from a plain program's by a relative error of at most 0.005.
Values may be sent and summed in bfloat16 or wider, within the bound.
No kernel may reach another device: no remote copies, remote signals or barrier semaphores. Data moves between devices by JAX's collectives and lax.ppermute only.
A program may use at most 64 MiB of HBM per device.

v0:
```python
import math
import jax
import jax.numpy as jnp
from jax import lax
from jax.sharding import PartitionSpec as P

INV_ROOT_TWO = 0.7071067811865476
INV_ROOT_TWO_PI = 0.3989422804014327


def gelu_value(values):
    return 0.5 * values * (1.0 + lax.erf(values * INV_ROOT_TWO))


def gelu_slope(values):
    normal_cdf = 0.5 * (1.0 + lax.erf(values * INV_ROOT_TWO))
    density = jnp.exp(-0.5 * values * values) * INV_ROOT_TWO_PI
    return normal_cdf + values * density


def contract_rows(left, right):
    return lax.dot_general(
        left, right, (((0,), (0,)), ((), ())), preferred_element_type=jnp.float32
    )


def contract_cols(left, right):
    return lax.dot_general(
        left, right, (((1,), (1,)), ((), ())), preferred_element_type=jnp.float32
    )


def on_device(inputs, out_grad, preact, first_weight, second_weight):
    pre_rows = lax.all_gather(preact, "row", axis=0, tiled=True)
    pre_whole = pre_rows.astype(jnp.float32)
    activated = gelu_value(pre_whole).astype(jnp.bfloat16)
    input_whole, grad_whole = (
        lax.all_gather(inputs, "col", axis=0, tiled=True),
        lax.all_gather(out_grad, "col", axis=0, tiled=True),
    )
    tokens_all = grad_whole.shape[0]
    factor = 1.0 / math.sqrt(tokens_all)
    token_rows = grad_whole
    grad_act = lax.psum_scatter(
        contract_cols(token_rows, second_weight), "row", scatter_dimension=0, tiled=True
    )
    grad_own = (grad_act * gelu_slope(preact.astype(jnp.float32))).astype(jnp.bfloat16)
    grad_pre = lax.all_gather(grad_own, "row", axis=0, tiled=True)
    grad_second = (contract_rows(activated, grad_whole) * factor).astype(jnp.bfloat16)
    first_total = contract_rows(input_whole, grad_pre)
    grad_first = (first_total * factor).astype(jnp.bfloat16)
    token_rows = grad_pre
    grad_inputs = lax.psum_scatter(
        contract_cols(token_rows, first_weight), "col", scatter_dimension=0, tiled=True
    )
    return (grad_inputs, grad_first, grad_second)


def solution(mesh):
    placed = (P("col", "row"), P("col", "row"), P("row", "col"), P("row", "col"), P("col", "row"))
    return jax.shard_map(
        on_device,
        mesh=mesh,
        in_specs=placed,
        out_specs=(P("col", "row"), P("row", "col"), P("col", "row")),
        check_vma=False,
    )
```

profile of v0, /device:TPU:8, one launch (start us, length us, event | category | flops | bytes accessed | tf_op | source)
XLA Modules:
  0.0 587.4 jit_solution(5867927629394080339)
XLA Ops:
  7.2 0.0 all-gather.5.cloned.1.call-start
  7.2 0.7 all-gather.5.cloned.1.call-update
  7.9 0.0 reduce-scatter.3.cloned.1.call-start
  8.0 64.7 %all-gather.5.cloned.1.call-done = bf16[1024,1152]{1,0:T(8,128)(2,1)} async-done(((bf16[32,1152]{1,0:T(8,128)(2,1)}), bf16[1024,1152]{1,0:T(8,128)(2,1)}) %all-gather.5.cloned.1.call-update) | async-done | bytes 2359312 | tf_op jit(solution)/shard_map/all_gather | solution.py:39
  72.7 7.3 %fusion.22 = f32[1024,1152]{1,0:T(8,128)} fusion(bf16[1024,1152]{1,0:T(8,128)(2,1)} %all-gather.5.cloned.1.call-done, bf16[1152,1152]{1,0:T(8,128)(2,1)S(1)} %copy-done), kind=kOutput, calls=%fused_computation.29 | convolution fusion | flops 2717908992 | bytes 9732096 | tf_op jit(solution)/shard_map/dot_general | solution.py:28
  80.0 0.0 reduce-scatter.3.cloned.1.call-update
  80.0 0.0 all-gather.7.cloned.1.call-start
  80.1 130.6 %reduce-scatter.3.cloned.1.call-done = f32[128,1152]{1,0:T(8,128)} async-done(((f32[1024,1152]{1,0:T(8,128)}), f32[128,1152]{1,0:T(8,128)}) %reduce-scatter.3.cloned.1.call-update) | async-done | bytes 589840 | tf_op jit(solution)/shard_map/reduce_scatter | solution.py:44
  210.7 2.0 fusion.18
  212.7 0.0 all-gather.7.cloned.1.call-update
  212.7 0.0 all-gather.11.cloned.1.call-start
  212.8 0.5 all-gather.11.cloned.1.call-update
  213.3 0.0 all-gather.9.cloned.1.call-start
  213.4 0.5 all-gather.9.cloned.1.call-update
  213.9 0.2 reduce-scatter.5.cloned.1.call-start
  214.1 75.9 %all-gather.7.cloned.1.call-done = bf16[1024,1152]{1,0:T(8,128)(2,1)} async-done(((bf16[128,1152]{1,0:T(8,128)(2,1)}), bf16[1024,1152]{1,0:T(8,128)(2,1)}) %all-gather.7.cloned.1.call-update) | async-done | bytes 2359312 | tf_op jit(solution)/shard_map/all_gather | solution.py:48
  290.1 8.1 %fusion.23 = f32[1024,1152]{1,0:T(8,128)} fusion(bf16[1024,1152]{1,0:T(8,128)(2,1)} %all-gather.7.cloned.1.call-done, bf16[1152,1152]{1,0:T(8,128)(2,1)} %param.8), kind=kOutput, calls=%fused_computation.30 | convolution fusion | flops 2717908992 | bytes 9732096 | tf_op jit(solution)/shard_map/dot_general | solution.py:28
  298.2 0.0 reduce-scatter.5.cloned.1.call-update
  298.2 69.9 %all-gather.11.cloned.1.call-done = bf16[1024,1152]{1,0:T(8,128)(2,1)} async-done(((bf16[128,1152]{1,0:T(8,128)(2,1)}), bf16[1024,1152]{1,0:T(8,128)(2,1)}) %all-gather.11.cloned.1.call-update) | async-done | bytes 2359312 | tf_op jit(solution)/shard_map/all_gather | solution.py:34
  368.2 7.2 %fusion.1 = bf16[1152,1152]{1,0:T(8,128)(2,1)} fusion(bf16[1024,1152]{1,0:T(8,128)(2,1)} %all-gather.5.cloned.1.call-done, bf16[1024,1152]{1,0:T(8,128)(2,1)} %all-gather.11.cloned.1.call-done), kind=kOutput, calls=%fused_computation.3 | convolution fusion | flops 2727641088 | bytes 7372800 | tf_op jit(solution)/shard_map/dot_general | solution.py:22
  375.4 50.3 %all-gather.9.cloned.1.call-done = bf16[1024,1152]{1,0:T(8,128)(2,1)} async-done(((bf16[32,1152]{1,0:T(8,128)(2,1)}), bf16[1024,1152]{1,0:T(8,128)(2,1)}) %all-gather.9.cloned.1.call-update) | async-done | bytes 2359312 | tf_op jit(solution)/shard_map/all_gather | solution.py:38
  425.7 7.2 %fusion.2 = bf16[1152,1152]{0,1:T(8,128)(2,1)} fusion(bf16[1024,1152]{1,0:T(8,128)(2,1)} %all-gather.7.cloned.1.call-done, bf16[1024,1152]{1,0:T(8,128)(2,1)} %all-gather.9.cloned.1.call-done), kind=kOutput, calls=%fused_computation.4 | convolution fusion | flops 2720563200 | bytes 7372800 | tf_op jit(solution)/shard_map/dot_general | solution.py:22
  432.8 5.2 copy.8
  438.1 142.5 %reduce-scatter.5.cloned.1.call-done = f32[32,1152]{1,0:T(8,128)} async-done(((f32[1024,1152]{1,0:T(8,128)}), f32[32,1152]{1,0:T(8,128)}) %reduce-scatter.5.cloned.1.call-update) | async-done | bytes 147472 | tf_op jit(solution)/shard_map/reduce_scatter | solution.py:53
  (4 shorter events, 0.0 us)
Async XLA Ops:
  7.2 65.5 %copy-start = (bf16[1152,1152]{1,0:T(8,128)(2,1)S(1)}, bf16[1152,1152]{1,0:T(8,128)(2,1)}, u32[]{:S(2)}) copy-start(bf16[1152,1152]{1,0:T(8,128)(2,1)} %param.9) | copy-start | bytes 7962628
  7.2 65.5 %all-gather.5.cloned.1.call-start = ((), (), s32[]{:S(2)}) async-start(), calls=%async_computation.2 | async-start | bytes 2433024 | tf_op jit(solution)/shard_map/all_gather | solution.py:39
  7.9 202.8 %reduce-scatter.3.cloned.1.call-start = ((), (), s32[]{:S(2)}) async-start(), calls=%async_computation.3 | async-start | bytes 5308416 | tf_op jit(solution)/shard_map/reduce_scatter | solution.py:44
  80.0 130.7 %copy-start.1 = (bf16[128,1152]{1,0:T(8,128)(2,1)S(1)}, bf16[128,1152]{1,0:T(8,128)(2,1)}, u32[]{:S(2)}) copy-start(bf16[128,1152]{1,0:T(8,128)(2,1)} %param.7) | copy-start | bytes 884740
  80.0 210.0 %all-gather.7.cloned.1.call-start = ((), (), s32[]{:S(2)}) async-start(), calls=%async_computation.4 | async-start | bytes 2654208 | tf_op jit(solution)/shard_map/all_gather | solution.py:48
  212.7 155.4 %all-gather.11.cloned.1.call-start = ((), (), s32[]{:S(2)}) async-start(), calls=%async_computation.7 | async-start | bytes 2654208 | tf_op jit(solution)/shard_map/all_gather | solution.py:34
  213.3 212.3 %all-gather.9.cloned.1.call-start = ((), (), s32[]{:S(2)}) async-start(), calls=%async_computation.6 | async-start | bytes 2433024 | tf_op jit(solution)/shard_map/all_gather | solution.py:38
  213.9 366.7 %reduce-scatter.5.cloned.1.call-start = ((), (), s32[]{:S(2)}) async-start(), calls=%async_computation.5 | async-start | bytes 4866048 | tf_op jit(solution)/shard_map/reduce_scatter | solution.py:53
Sparse Core Ops, SparseCore 0:
  9.8 62.8 all-gather.4
  80.2 130.4 reduce-scatter.2
  213.9 76.1 all-gather.6
  292.5 75.5 all-gather.10
  369.9 55.7 all-gather.8
  428.6 151.8 reduce-scatter.4
where the time goes:
time: 588 us; the launch traced here: 587 us
  waiting for transfers between devices  536 us (91%)
  matrix products  29.8 us (5%)
  between operations  14.1 us (2%)
    reduce_scatter x1, waiting for transfers between devices, on_device(): lax.psum_scatter(contract_cols(token_rows, first_weight), 'col', scatter_...  143 us
    reduce_scatter x1, waiting for transfers between devices, on_device(): lax.psum_scatter(contract_cols(token_rows, second_weight), 'row', scatter...  131 us
    all_gather x1, waiting for transfers between devices, on_device(): grad_pre = lax.all_gather(grad_own, 'row', axis=0, tiled=True)  75.9 us
    all_gather x1, waiting for transfers between devices, on_device(): pre_rows = lax.all_gather(preact, 'row', axis=0, tiled=True)  69.9 us
    all_gather x1, waiting for transfers between devices, on_device(): lax.all_gather(out_grad, 'col', axis=0, tiled=True)  64.7 us
    all_gather x1, waiting for transfers between devices, on_device(): lax.all_gather(inputs, 'col', axis=0, tiled=True)  50.3 us
    dot_general x2, matrix products, contract_cols(): lax.dot_general(left, right, (((1,), (1,)), ((), ())), preferred_element_...  15.4 us
    dot_general x2, matrix products, contract_rows(): lax.dot_general(left, right, (((0,), (0,)), ((), ())), preferred_element_...  14.4 us
  transfers between devices with their start and end apart: 6, of which 6 were waited for; matrix products, arithmetic and copies ran while one was open for 5% of the time, Pallas kernels for 0%

commit v1 on v0

--- a/solution.py
+++ b/solution.py
@@ -35,7 +35,9 @@
     pre_whole = pre_rows.astype(jnp.float32)
     activated = gelu_value(pre_whole).astype(jnp.bfloat16)
     input_whole, grad_whole = (
-        lax.all_gather(inputs, "col", axis=0, tiled=True),
+        jnp.concatenate(
+            lax.all_to_all(jnp.stack([inputs] * lax.axis_size("col")), "col", 0, 0), axis=0
+        ),
         lax.all_gather(out_grad, "col", axis=0, tiled=True),
     )
     tokens_all = grad_whole.shape[0]

time: 588 us -> 543 us (0.923)
  waiting for transfers between devices: 536 us -> 484 us
    all_gather x1 -> x0, waiting for transfers between devices: 50.3 us -> none  [on_device(): lax.all_gather(inputs, 'col', axis=0, tiled=True)]
    reduce_scatter x1, waiting for transfers between devices: 143 us -> 132 us  [on_device(): lax.psum_scatter(contract_cols(token_rows, first_weight), 'col', scatter_...]
    all_gather x1, waiting for transfers between devices: 69.9 us -> 78.7 us  [on_device(): pre_rows = lax.all_gather(preact, 'row', axis=0, tiled=True)]
  transfers between devices with their start and end apart: 6 -> 6, of which waited for: 6 -> 5; matrix products, arithmetic and copies ran while one was open for 5% -> 5% of each run, Pallas kernels for 0% -> 0%
where the time goes in v1:
time: 543 us
  waiting for transfers between devices  484 us (89%)
  matrix products  29.8 us (5%)
  between operations  13.8 us (3%)
  local copies, waits for them, and re-layouts  7.67 us (1%)
    reduce_scatter x1, waiting for transfers between devices, on_device(): lax.psum_scatter(contract_cols(token_rows, first_weight), 'col', scatter_...  132 us
    reduce_scatter x1, waiting for transfers between devices, on_device(): lax.psum_scatter(contract_cols(token_rows, second_weight), 'row', scatter...  131 us
    all_gather x1, waiting for transfers between devices, on_device(): pre_rows = lax.all_gather(preact, 'row', axis=0, tiled=True)  78.7 us
    all_gather x1, waiting for transfers between devices, on_device(): grad_pre = lax.all_gather(grad_own, 'row', axis=0, tiled=True)  76.7 us
    all_gather x1, waiting for transfers between devices, on_device(): lax.all_gather(out_grad, 'col', axis=0, tiled=True)  64.7 us
    dot_general x2, matrix products, contract_cols(): lax.dot_general(left, right, (((1,), (1,)), ((), ())), preferred_element_...  15.4 us
    dot_general x2, matrix products, contract_rows(): lax.dot_general(left, right, (((0,), (0,)), ((), ())), preferred_element_...  14.4 us
  transfers between devices with their start and end apart: 6, of which 5 were waited for; matrix products, arithmetic and copies ran while one was open for 5% of the time, Pallas kernels for 0%

profile of v1, /device:TPU:8, one launch (start us, length us, event | category | flops | bytes accessed | tf_op | source)
XLA Modules:
  0.0 542.8 jit_solution(15688213987794432362)
XLA Ops:
  7.2 0.0 all-gather.4.cloned.1.call-start
  7.2 0.7 all-gather.4.cloned.1.call-update
  7.9 0.0 reduce-scatter.3.cloned.1.call-start
  8.0 64.7 %all-gather.4.cloned.1.call-done = bf16[1024,1152]{1,0:T(8,128)(2,1)} async-done(((bf16[32,1152]{1,0:T(8,128)(2,1)}), bf16[1024,1152]{1,0:T(8,128)(2,1)}) %all-gather.4.cloned.1.call-update) | async-done | bytes 2359312 | tf_op jit(solution)/shard_map/all_gather | solution.py:41
  72.7 7.3 %fusion.22 = f32[1024,1152]{1,0:T(8,128)} fusion(bf16[1024,1152]{1,0:T(8,128)(2,1)} %all-gather.4.cloned.1.call-done, bf16[1152,1152]{1,0:T(8,128)(2,1)S(1)} %copy-done), kind=kOutput, calls=%fused_computation.29 | convolution fusion | flops 2717908992 | bytes 9732096 | tf_op jit(solution)/shard_map/dot_general | solution.py:28
  80.0 0.0 reduce-scatter.3.cloned.1.call-update
  80.0 0.0 all-gather.6.cloned.1.call-start
  80.1 130.6 %reduce-scatter.3.cloned.1.call-done = f32[128,1152]{1,0:T(8,128)} async-done(((f32[1024,1152]{1,0:T(8,128)}), f32[128,1152]{1,0:T(8,128)}) %reduce-scatter.3.cloned.1.call-update) | async-done | bytes 589840 | tf_op jit(solution)/shard_map/reduce_scatter | solution.py:46
  210.7 2.0 fusion.18
  212.7 0.0 all-gather.6.cloned.1.call-update
  212.7 0.0 all-gather.8.cloned.1.call-start
  212.8 0.5 all-gather.8.cloned.1.call-update
  213.3 0.0 reduce-scatter.5.cloned.1.call-start
  213.4 76.7 %all-gather.6.cloned.1.call-done = bf16[1024,1152]{1,0:T(8,128)(2,1)} async-done(((bf16[128,1152]{1,0:T(8,128)(2,1)}), bf16[1024,1152]{1,0:T(8,128)(2,1)}) %all-gather.6.cloned.1.call-update) | async-done | bytes 2359312 | tf_op jit(solution)/shard_map/all_gather | solution.py:50
  290.1 8.1 %fusion.23 = f32[1024,1152]{1,0:T(8,128)} fusion(bf16[1024,1152]{1,0:T(8,128)(2,1)} %all-gather.6.cloned.1.call-done, bf16[1152,1152]{1,0:T(8,128)(2,1)} %param.8), kind=kOutput, calls=%fused_computation.30 | convolution fusion | flops 2717908992 | bytes 9732096 | tf_op jit(solution)/shard_map/dot_general | solution.py:28
  298.2 0.0 reduce-scatter.5.cloned.1.call-update
  298.2 0.9 copy-done.2
  299.1 1.6 stack.2
  300.6 5.0 all-to-all-start
  305.6 78.7 %all-gather.8.cloned.1.call-done = bf16[1024,1152]{1,0:T(8,128)(2,1)} async-done(((bf16[128,1152]{1,0:T(8,128)(2,1)}), bf16[1024,1152]{1,0:T(8,128)(2,1)}) %all-gather.8.cloned.1.call-update) | async-done | bytes 2359312 | tf_op jit(solution)/shard_map/all_gather | solution.py:34
  384.4 7.2 %fusion.1 = bf16[1152,1152]{1,0:T(8,128)(2,1)} fusion(bf16[1024,1152]{1,0:T(8,128)(2,1)} %all-gather.4.cloned.1.call-done, bf16[1024,1152]{1,0:T(8,128)(2,1)} %all-gather.8.cloned.1.call-done), kind=kOutput, calls=%fused_computation.3 | convolution fusion | flops 2727641088 | bytes 7372800 | tf_op jit(solution)/shard_map/dot_general | solution.py:22
  391.6 7.2 %fusion.2 = bf16[1152,1152]{0,1:T(8,128)(2,1)} fusion(bf16[1024,1152]{1,0:T(8,128)(2,1)} %all-gather.6.cloned.1.call-done, bf16[1024,1152]{1,0:T(8,128)(2,1)} %bitcast), kind=kOutput, calls=%fused_computation.4 | convolution fusion | flops 2720563200 | bytes 7372800 | tf_op jit(solution)/shard_map/dot_general | solution.py:22
  398.7 5.2 copy.8
  404.0 132.3 %reduce-scatter.5.cloned.1.call-done = f32[32,1152]{1,0:T(8,128)} async-done(((f32[1024,1152]{1,0:T(8,128)}), f32[32,1152]{1,0:T(8,128)}) %reduce-scatter.5.cloned.1.call-update) | async-done | bytes 147472 | tf_op jit(solution)/shard_map/reduce_scatter | solution.py:55
  (6 shorter events, 0.0 us)
Async XLA Ops:
  7.2 65.5 %copy-start = (bf16[1152,1152]{1,0:T(8,128)(2,1)S(1)}, bf16[1152,1152]{1,0:T(8,128)(2,1)}, u32[]{:S(2)}) copy-start(bf16[1152,1152]{1,0:T(8,128)(2,1)} %param.9) | copy-start | bytes 7962628
  7.2 65.5 %all-gather.4.cloned.1.call-start = ((), (), s32[]{:S(2)}) async-start(), calls=%async_computation.3 | async-start | bytes 2433024 | tf_op jit(solution)/shard_map/all_gather | solution.py:41
  7.9 202.8 %reduce-scatter.3.cloned.1.call-start = ((), (), s32[]{:S(2)}) async-start(), calls=%async_computation.4 | async-start | bytes 5308416 | tf_op jit(solution)/shard_map/reduce_scatter | solution.py:46
  80.0 130.7 %copy-start.1 = (bf16[128,1152]{1,0:T(8,128)(2,1)S(1)}, bf16[128,1152]{1,0:T(8,128)(2,1)}, u32[]{:S(2)}) copy-start(bf16[128,1152]{1,0:T(8,128)(2,1)} %param.7) | copy-start | bytes 884740
  80.0 210.0 %all-gather.6.cloned.1.call-start = ((), (), s32[]{:S(2)}) async-start(), calls=%async_computation.5 | async-start | bytes 2654208 | tf_op jit(solution)/shard_map/all_gather | solution.py:50
  212.7 171.6 %all-gather.8.cloned.1.call-start = ((), (), s32[]{:S(2)}) async-start(), calls=%async_computation.7 | async-start | bytes 2654208 | tf_op jit(solution)/shard_map/all_gather | solution.py:34
  213.3 323.0 %reduce-scatter.5.cloned.1.call-start = ((), (), s32[]{:S(2)}) async-start(), calls=%async_computation.6 | async-start | bytes 4866048 | tf_op jit(solution)/shard_map/reduce_scatter | solution.py:55
  298.2 0.9 copy-start.2
  300.6 90.9 %all-to-all-start = ((bf16[32,32,1152]{2,1,0:T(8,128)(2,1)}), bf16[32,32,1152]{2,1,0:T(8,128)(2,1)}, u32[]{:S(2)}, u32[]{:S(2)}) async-start(bf16[32,32,1152]{2,1,0:T(8,128)(2,1)} %stack.2), calls=%async_computation.2 | async-start | bytes 4718592 | tf_op jit(solution)/shard_map/all_to_all | solution.py:39
Sparse Core Ops, SparseCore 0:
  9.8 62.8 all-gather.3
  80.2 130.4 reduce-scatter.2
  213.9 76.1 all-gather.5
  292.5 91.7 all-gather.7
  387.3 148.9 reduce-scatter.4
